TPU v7x, 32 devices: a whole 2x2x4 slice. The times are simulated.
32 devices in a mesh: groups: 2 (over x), seq: 16 (over z, y, core).
Axes of the slice: x: 2, y: 2, z: 4, core: 2. Of those that a mesh axis runs over, the one named last changes fastest.
Arguments:
- hidden: bfloat16 [16384, 320], P(('groups', 'seq')), parts along dimension 0, may hold values from -20 to 20
- ref_hidden: bfloat16 [2048, 320], P(('groups', 'seq')), parts along dimension 0, may hold values from -6 to 6
- visible: int32 [128, 64], P('groups'), parts along dimension 0, may hold values 0 or 1
- ref_count: int32 [2], P('groups'), parts along dimension 0, may hold values from 256 to 1024
- w_query: bfloat16 [320, 320], replicated, may hold values from -0.3125 to 0.3125
- w_key: bfloat16 [320, 320], replicated, may hold values from -0.3125 to 0.3125
- w_value: bfloat16 [320, 320], replicated, may hold values from -0.3125 to 0.3125
- w_out: bfloat16 [320, 320], replicated, may hold values from -0.3125 to 0.3125
Outputs:
- attended: bfloat16 [16384, 320], P(('groups', 'seq')), parts along dimension 0
There are 2 independent parts, one for each index of `groups`. A program takes and returns all parts, laid end to end along the dimension named above; an argument that names none is the same for every part. Nothing has to cross between parts.
All inputs are finite; a program needn't handle non-finite values.
Results may differ from a plain program's by a relative error of at most 0.011.
Values may be sent and summed in bfloat16 or wider, within the bound.
A program may use at most 128 MiB of HBM per device.

v0:
```python
import math
import jax
import jax.numpy as jnp
from jax import lax
from jax.sharding import PartitionSpec as P

HEADS = 5
TILE = 128
TILES_VIEW = 8


def project(states, weight, head_count):
    result = jnp.dot(states, weight, preferred_element_type=jnp.float32).astype(jnp.bfloat16)
    return result.reshape(states.shape[0], head_count, weight.shape[1] // head_count)


def local(hidden, ref_hidden, visible, ref_count, w_query, w_key, w_value, w_out):
    row_count = hidden.shape[0]
    width = hidden.shape[1]
    head_count = HEADS
    head_size = width // head_count
    scale = 1.0 / math.sqrt(head_size)
    tile_count = visible.shape[0]
    view_tiles = TILES_VIEW
    row_start = lax.axis_index("seq") * row_count
    queries = project(hidden, w_query, head_count)
    row_tile = (row_start + jnp.arange(row_count, dtype=jnp.int32)) // TILE
    row_view = row_tile // view_tiles
    picker = (row_tile[:, None] == jnp.arange(tile_count, dtype=jnp.int32)[None, :]).astype(
        jnp.float32
    )
    seen_tiles = jnp.dot(picker, visible.astype(jnp.float32))

    def attend(state, key_rows, value_rows, allowed):
        run_max, run_total, run_acc = state
        scores = (
            jnp.einsum("qhd,khd->hqk", queries, key_rows, preferred_element_type=jnp.float32)
            * scale
        )
        scores = jnp.where(allowed[None, :, :], scores, jnp.float32(-1e30))
        new_max = jnp.maximum(run_max, jnp.max(scores, axis=-1))
        expo = jnp.exp(scores - new_max[:, :, None])
        factor = jnp.exp(run_max - new_max)
        new_total = run_total * factor + jnp.sum(expo, axis=-1)
        new_acc = run_acc * factor[:, :, None] + jnp.einsum(
            "hqk,khd->hqd",
            expo.astype(jnp.bfloat16),
            value_rows,
            preferred_element_type=jnp.float32,
        )
        return (new_max, new_total, new_acc)

    def view_block(state, key_rows, value_rows, offset):
        key_count = key_rows.shape[0]
        key_tile = (offset + jnp.arange(key_count, dtype=jnp.int32)) // TILE
        onehot = (key_tile[:, None] == jnp.arange(tile_count, dtype=jnp.int32)[None, :]).astype(
            jnp.float32
        )
        tile_hits = jnp.dot(seen_tiles, onehot.T)
        allowed = (tile_hits > 0.5) | (row_view[:, None] == (key_tile // view_tiles)[None, :])
        return attend(state, key_rows, value_rows, allowed)

    local_keys = jnp.dot(ref_hidden, w_key, preferred_element_type=jnp.float32).astype(jnp.bfloat16)
    local_values = jnp.dot(ref_hidden, w_value, preferred_element_type=jnp.float32).astype(
        jnp.bfloat16
    )
    ref_keys, ref_values = (
        lax.all_gather(local_keys, "seq", axis=0, tiled=True),
        lax.all_gather(local_values, "seq", axis=0, tiled=True),
    )
    ref_keys = ref_keys.reshape(ref_keys.shape[0], head_count, head_size)
    ref_values = ref_values.reshape(ref_values.shape[0], head_count, head_size)
    ref_total = ref_keys.shape[0]
    ref_allowed = jnp.broadcast_to(
        (jnp.arange(ref_total, dtype=jnp.int32) < ref_count[0])[None, :], (row_count, ref_total)
    )
    initial = (
        jnp.full((head_count, row_count), -1e30, jnp.float32),
        jnp.zeros((head_count, row_count), jnp.float32),
        jnp.zeros((head_count, row_count, head_size), jnp.float32),
    )
    state = attend(initial, ref_keys, ref_values, ref_allowed)
    view_keys = project(hidden, w_key, head_count)
    view_values = project(hidden, w_value, head_count)
    pieces = (
        lax.all_gather(view_keys, "seq", axis=0, tiled=True),
        lax.all_gather(view_values, "seq", axis=0, tiled=True),
    )
    sweep_state = state
    key_rows = pieces[0]
    value_rows = pieces[1]
    key_count = key_rows.shape[0]
    block_size = 512
    block_count = key_count // block_size
    key_blocks = key_rows.reshape(block_count, block_size, head_count, head_size)
    value_blocks = value_rows.reshape(block_count, block_size, head_count, head_size)

    def advance(inner, pieces):
        block_index, key_part, value_part = pieces
        return (view_block(inner, key_part, value_part, block_index * block_size), None)

    sweep_state, unused = lax.scan(
        advance, sweep_state, (jnp.arange(block_count, dtype=jnp.int32), key_blocks, value_blocks)
    )
    state = sweep_state
    run_max, run_total, run_acc = state
    mixed = run_acc / run_total[:, :, None]
    mixed = jnp.transpose(mixed, (1, 0, 2)).reshape(row_count, width).astype(jnp.bfloat16)
    return jnp.dot(mixed, w_out, preferred_element_type=jnp.float32).astype(jnp.bfloat16)


def solution(mesh):
    in_specs = (
        P(("groups", "seq"), None),
        P(("groups", "seq"), None),
        P("groups", None),
        P("groups"),
        P(),
        P(),
        P(),
        P(),
    )
    out_specs = P(("groups", "seq"), None)
    return jax.shard_map(local, mesh=mesh, in_specs=in_specs, out_specs=out_specs, check_vma=False)
```

profile of v0, /device:TPU:0, one launch (start us, length us, event | category | flops | bytes accessed | tf_op | source)
XLA Modules:
  0.0 273.2 jit_solution(13204093446191117111)
XLA Ops:
  13.5 28.4 %all_gather.12 = bf16[1024,320]{1,0:T(8,128)(2,1)S(1)} all-gather(bf16[64,320]{1,0:T(8,128)(2,1)S(1)} %convolution_convert_fusion.5), channel_id=1, replica_groups=mesh['groups'=2,'seq'=16] {'seq'}, dimensions={0}, use_global_device_ids=true | all-gather | bytes 696320 | tf_op jit(solution)/shard_map/all_gather | solution.py:68
  43.3 24.3 %all_gather.13 = bf16[1024,320]{1,0:T(8,128)(2,1)S(1)} all-gather(bf16[64,320]{1,0:T(8,128)(2,1)S(1)} %convolution_convert_fusion.4), channel_id=1, replica_groups=mesh['groups'=2,'seq'=16] {'seq'}, dimensions={0}, use_global_device_ids=true | all-gather | bytes 696320 | tf_op jit(solution)/shard_map/all_gather | solution.py:69
  69.9 2.5 fusion.35
  75.0 4.0 %all-gather.5.cloned.1.call-done = bf16[8192,5,64]{0,2,1:T(8,128)(2,1)} async-done(((bf16[512,5,64]{0,2,1:T(8,128)(2,1)}), bf16[8192,5,64]{0,2,1:T(8,128)(2,1)}) %all-gather.5.cloned.1.call-update) | async-done | bytes 5242896 | tf_op jit(solution)/shard_map/all_gather | solution.py:87
  79.0 5.6 %copy.25 = bf16[5,8,16,8,512]{4,3,1,0,2:T(8,128)(2,1)} copy(bf16[5,8,16,8,512]{4,3,2,1,0:T(8,128)(2,1)} %bitcast.81) | data formatting | bytes 10485760 | tf_op jit(solution)/shard_map/reshape | solution.py:96
  84.6 56.0 %all-gather.3.cloned.1.call-done = bf16[8192,5,64]{0,2,1:T(8,128)(2,1)} async-done(((bf16[512,5,64]{0,2,1:T(8,128)(2,1)}), bf16[8192,5,64]{0,2,1:T(8,128)(2,1)}) %all-gather.3.cloned.1.call-update) | async-done | bytes 5242896 | tf_op jit(solution)/shard_map/all_gather | solution.py:86
  140.6 5.6 %copy.26 = bf16[5,8,16,8,512]{4,3,1,0,2:T(8,128)(2,1)} copy(bf16[5,8,16,8,512]{4,3,2,1,0:T(8,128)(2,1)} %bitcast.82) | data formatting | bytes 10485760 | tf_op jit(solution)/shard_map/reshape | solution.py:95
  146.2 118.9 %while.18 = (s32[]{:T(128)}, f32[5,512]{1,0:T(8,128)S(1)}, f32[5,512]{1,0:T(8,128)S(1)}, f32[5,512,64]{1,2,0:T(8,128)S(1)}, s32[16]{0:T(128)S(1)}, /*index=5*/bf...) while((s32[]{:T(128)}, f32[5,512]{1,0:T(8,128)S(1)}, ...), condition=%wide.region_5.6_spmd.clone, body=%wide.region_2.5_spmd.clone.sunk | while | flops 384700416 | bytes 19313812 | solution.py:102
  151.1 2.5 fusion.83
  158.5 2.5 fusion.83
  166.0 2.5 fusion.83
  173.4 2.5 fusion.83
  180.8 2.5 fusion.83
  188.3 2.5 fusion.83
  195.7 2.5 fusion.83
  203.1 2.5 fusion.83
  210.6 2.5 fusion.83
  218.0 2.5 fusion.83
  225.4 2.5 fusion.83
  232.9 2.5 fusion.83
  240.3 2.5 fusion.83
  247.7 2.5 fusion.83
  255.2 2.5 fusion.83
  262.6 2.5 fusion.83
  (173 shorter events, 80.5 us)
Async XLA Ops:
  6.5 1.0 copy-start
  6.5 61.3 %copy-start.1 = (bf16[320,320]{1,0:T(8,128)(2,1)S(1)}, bf16[320,320]{1,0:T(8,128)(2,1)}, u32[]{:S(2)}) copy-start(bf16[320,320]{1,0:T(8,128)(2,1)} %param.14) | copy-start | bytes 614404
  6.5 72.5 %all-gather.5.cloned.1.call-start = ((), (), s32[]{:S(2)}) async-start(), calls=%async_computation.1 | async-start | bytes 5570560 | tf_op jit(solution)/shard_map/all_gather | solution.py:87
  9.6 131.1 %all-gather.3.cloned.1.call-start = ((), (), s32[]{:S(2)}) async-start(), calls=%async_computation | async-start | bytes 5570560 | tf_op jit(solution)/shard_map/all_gather | solution.py:86
  69.9 2.5 copy-start.3
  146.2 119.0 %copy-start.2 = (bf16[320,320]{1,0:T(8,128)(2,1)S(1)}, bf16[320,320]{1,0:T(8,128)(2,1)}, u32[]{:S(2)}) copy-start(bf16[320,320]{1,0:T(8,128)(2,1)} %param.17) | copy-start | bytes 614404
Sparse Core Ops, SparseCore 0:
  9.7 69.3 all-gather.4
  81.2 59.3 all-gather.2
where the time goes:
time: 275 us; the launch traced here: 273 us
  matrix products  91.4 us (33%)
  waiting for transfers between devices  60.1 us (22%)
  blocking collectives  52.6 us (19%)
  local copies, waits for them, and re-layouts  22.1 us (8%)
  other arithmetic  21.1 us (8%)
  between operations  14.2 us (5%)
  loops' own time  11.7 us (4%)
    all_gather x1, waiting for transfers between devices, local(): lax.all_gather(view_keys, 'seq', axis=0, tiled=True)  56 us
    dot_general x17, matrix products, attend(): jnp.einsum('hqk,khd->hqd', expo.astype(jnp.bfloat16), value_rows, preferr...  42.9 us
    dot_general x17, matrix products, attend(): jnp.einsum('qhd,khd->hqk', queries, key_rows, preferred_element_type=jnp....  34.2 us
    all_gather x1, blocking collectives, local(): lax.all_gather(local_keys, 'seq', axis=0, tiled=True)  28.4 us
    all_gather x1, blocking collectives, local(): lax.all_gather(local_values, 'seq', axis=0, tiled=True)  24.3 us
    reduce_sum x17, other arithmetic, attend(): new_total = run_total * factor + jnp.sum(expo, axis=-1)  20.1 us
    another operation x1, loops' own time, local(): lax.scan(advance, sweep_state, (jnp.arange(block_count, dtype=jnp.int32),...  11.7 us
    dynamic_slice x16, local copies, waits for them, and re-layouts, local(): lax.scan(advance, sweep_state, (jnp.arange(block_count, dtype=jnp.int32),...  9.38 us
  transfers between devices with their start and end apart: 2, of which 2 were waited for; matrix products, arithmetic and copies ran while one was open for 6% of the time, Pallas kernels for 0%

commit v1 on v0

--- a/solution.py
+++ b/solution.py
@@ -7,6 +7,19 @@
 HEADS = 5
 TILE = 128
 TILES_VIEW = 8
+
+
+def gather_around(array, axis, dim):
+    length, position, rows = (lax.axis_size(axis), lax.axis_index(axis), array.shape[dim])
+    upward = [(i, (i + 1) % length) for i in range(length)]
+    whole = jnp.zeros((*array.shape[:dim], length * rows, *array.shape[dim + 1 :]), array.dtype)
+    block = array
+    for lap in range(length):
+        source = (position - lap) % length
+        whole = lax.dynamic_update_slice_in_dim(whole, block, source * rows, axis=dim)
+        if lap < length - 1:
+            block = lax.ppermute(block, axis, upward)
+    return whole
 
 
 def project(states, weight, head_count):
@@ -65,7 +78,7 @@
         jnp.bfloat16
     )
     ref_keys, ref_values = (
-        lax.all_gather(local_keys, "seq", axis=0, tiled=True),
+        gather_around(local_keys, "seq", 0),
         lax.all_gather(local_values, "seq", axis=0, tiled=True),
     )
     ref_keys = ref_keys.reshape(ref_keys.shape[0], head_count, head_size)

time: 275 us -> 282 us (1.025)
  blocking collectives: 52.6 us -> 22.9 us
  waiting for transfers between devices: 60.1 us -> 83.8 us
  local copies, waits for them, and re-layouts: 22.1 us -> 32.5 us
    ppermute x0 -> x15, waiting for transfers between devices: none -> 83.7 us  [gather_around(): block = lax.ppermute(block, axis, upward)]
    all_gather x1, waiting for transfers between devices: 56 us -> 0.01 us  [local(): lax.all_gather(view_keys, 'seq', axis=0, tiled=True)]
    all_gather x1 -> x0, blocking collectives: 28.4 us -> none  [local(): lax.all_gather(local_keys, 'seq', axis=0, tiled=True)]
    dynamic_update_slice x0 -> x16, local copies, waits for them, and re-layouts: none -> 8.59 us  [gather_around(): lax.dynamic_update_slice_in_dim(whole, block, source * rows, axis=dim)]
    all_gather x1, waiting for transfers between devices: 4.02 us -> 0.02 us  [local(): lax.all_gather(view_values, 'seq', axis=0, tiled=True)]
  transfers between devices with their start and end apart: 2 -> 17, of which waited for: 2 -> 13; matrix products, arithmetic and copies ran while one was open for 6% -> 11% of each run, Pallas kernels for 0% -> 0%
where the time goes in v1:
time: 282 us; the launch traced here: 281 us
  matrix products  93.1 us (33%)
  waiting for transfers between devices  83.8 us (30%)
  local copies, waits for them, and re-layouts  32.5 us (12%)
  blocking collectives  22.9 us (8%)
  other arithmetic  21.1 us (7%)
  between operations  14.7 us (5%)
  loops' own time  11.7 us (4%)
    ppermute x15, waiting for transfers between devices, gather_around(): block = lax.ppermute(block, axis, upward)  83.7 us
    dot_general x17, matrix products, attend(): jnp.einsum('hqk,khd->hqd', expo.astype(jnp.bfloat16), value_rows, preferr...  42.9 us
    dot_general x17, matrix products, attend(): jnp.einsum('qhd,khd->hqk', queries, key_rows, preferred_element_type=jnp....  34.2 us
    all_gather x1, blocking collectives, local(): lax.all_gather(local_values, 'seq', axis=0, tiled=True)  22.9 us
    reduce_sum x17, other arithmetic, attend(): new_total = run_total * factor + jnp.sum(expo, axis=-1)  20.1 us
    another operation x1, loops' own time, local(): lax.scan(advance, sweep_state, (jnp.arange(block_count, dtype=jnp.int32),...  11.7 us
    dynamic_slice x16, local copies, waits for them, and re-layouts, local(): lax.scan(advance, sweep_state, (jnp.arange(block_count, dtype=jnp.int32),...  9.38 us
    dynamic_update_slice x16, local copies, waits for them, and re-layouts, gather_around(): lax.dynamic_update_slice_in_dim(whole, block, source * rows, axis=dim)  8.59 us
  transfers between devices with their start and end apart: 17, of which 13 were waited for; matrix products, arithmetic and copies ran while one was open for 11% of the time, Pallas kernels for 0%

profile of v1, /device:TPU:0, one launch (start us, length us, event | category | flops | bytes accessed | tf_op | source)
XLA Modules:
  0.0 280.6 jit_solution(7759170977460565810)
XLA Ops:
  13.4 6.8 %collective-permute-done = bf16[64,320]{1,0:T(8,128)(2,1)S(1)} collective-permute-done((bf16[64,320]{1,0:T(8,128)(2,1)S(1)}, bf16[64,320]{1,0:T(8,128)(2,1)S(1)}, u32[]{:S(2)}, u32[]{:S(2)}) %collective-permute-start) | collective-permute-done | bytes 40992 | tf_op jit(solution)/shard_map/ppermute | solution.py:21
  20.1 6.8 %collective-permute-done.1 = bf16[64,320]{1,0:T(8,128)(2,1)S(1)} collective-permute-done((bf16[64,320]{1,0:T(8,128)(2,1)S(1)}, bf16[64,320]{1,0:T(8,128)(2,1)S(1)}, u32[]{:S(2)}, u32[]{:S(2)}) %collective-permute-start.1) | collective-permute-done | bytes 40992 | tf_op jit(solution)/shard_map/ppermute | solution.py:21
  27.0 7.0 %collective-permute-done.2 = bf16[64,320]{1,0:T(8,128)(2,1)S(1)} collective-permute-done((bf16[64,320]{1,0:T(8,128)(2,1)S(1)}, bf16[64,320]{1,0:T(8,128)(2,1)S(1)}, u32[]{:S(2)}, u32[]{:S(2)}) %collective-permute-start.2) | collective-permute-done | bytes 40992 | tf_op jit(solution)/shard_map/ppermute | solution.py:21
  34.0 6.2 %collective-permute-done.3 = bf16[64,320]{1,0:T(8,128)(2,1)S(1)} collective-permute-done((bf16[64,320]{1,0:T(8,128)(2,1)S(1)}, bf16[64,320]{1,0:T(8,128)(2,1)S(1)}, u32[]{:S(2)}, u32[]{:S(2)}) %collective-permute-start.3) | collective-permute-done | bytes 40992 | tf_op jit(solution)/shard_map/ppermute | solution.py:21
  40.2 6.2 %collective-permute-done.4 = bf16[64,320]{1,0:T(8,128)(2,1)S(1)} collective-permute-done((bf16[64,320]{1,0:T(8,128)(2,1)S(1)}, bf16[64,320]{1,0:T(8,128)(2,1)S(1)}, u32[]{:S(2)}, u32[]{:S(2)}) %collective-permute-start.4) | collective-permute-done | bytes 40992 | tf_op jit(solution)/shard_map/ppermute | solution.py:21
  46.4 7.4 %collective-permute-done.5 = bf16[64,320]{1,0:T(8,128)(2,1)S(1)} collective-permute-done((bf16[64,320]{1,0:T(8,128)(2,1)S(1)}, bf16[64,320]{1,0:T(8,128)(2,1)S(1)}, u32[]{:S(2)}, u32[]{:S(2)}) %collective-permute-start.5) | collective-permute-done | bytes 40992 | tf_op jit(solution)/shard_map/ppermute | solution.py:21
  53.8 7.1 %collective-permute-done.6 = bf16[64,320]{1,0:T(8,128)(2,1)S(1)} collective-permute-done((bf16[64,320]{1,0:T(8,128)(2,1)S(1)}, bf16[64,320]{1,0:T(8,128)(2,1)S(1)}, u32[]{:S(2)}, u32[]{:S(2)}) %collective-permute-start.6) | collective-permute-done | bytes 40992 | tf_op jit(solution)/shard_map/ppermute | solution.py:21
  60.9 7.2 %collective-permute-done.7 = bf16[64,320]{1,0:T(8,128)(2,1)S(1)} collective-permute-done((bf16[64,320]{1,0:T(8,128)(2,1)S(1)}, bf16[64,320]{1,0:T(8,128)(2,1)S(1)}, u32[]{:S(2)}, u32[]{:S(2)}) %collective-permute-start.7) | collective-permute-done | bytes 40992 | tf_op jit(solution)/shard_map/ppermute | solution.py:21
  68.2 6.2 %collective-permute-done.8 = bf16[64,320]{1,0:T(8,128)(2,1)S(1)} collective-permute-done((bf16[64,320]{1,0:T(8,128)(2,1)S(1)}, bf16[64,320]{1,0:T(8,128)(2,1)S(1)}, u32[]{:S(2)}, u32[]{:S(2)}) %collective-permute-start.8) | collective-permute-done | bytes 40992 | tf_op jit(solution)/shard_map/ppermute | solution.py:21
  75.5 5.1 %collective-permute-done.9 = bf16[64,320]{1,0:T(8,128)(2,1)S(1)} collective-permute-done((bf16[64,320]{1,0:T(8,128)(2,1)S(1)}, bf16[64,320]{1,0:T(8,128)(2,1)S(1)}, u32[]{:S(2)}, u32[]{:S(2)}) %collective-permute-start.9) | collective-permute-done | bytes 40992 | tf_op jit(solution)/shard_map/ppermute | solution.py:21
  80.6 22.9 %all_gather.9 = bf16[1024,320]{1,0:T(8,128)(2,1)S(1)} all-gather(bf16[64,320]{1,0:T(8,128)(2,1)S(1)} %convolution_convert_fusion.4), channel_id=1, replica_groups=mesh['groups'=2,'seq'=16] {'seq'}, dimensions={0}, use_global_device_ids=true | all-gather | bytes 696320 | tf_op jit(solution)/shard_map/all_gather | solution.py:82
  105.0 4.7 %collective-permute-done.11 = bf16[64,320]{1,0:T(8,128)(2,1)S(1)} collective-permute-done((bf16[64,320]{1,0:T(8,128)(2,1)S(1)}, bf16[64,320]{1,0:T(8,128)(2,1)S(1)}, u32[]{:S(2)}, u32[]{:S(2)}) %collective-permute-start.11) | collective-permute-done | bytes 40992 | tf_op jit(solution)/shard_map/ppermute | solution.py:21
  109.8 7.4 %collective-permute-done.12 = bf16[64,320]{1,0:T(8,128)(2,1)S(1)} collective-permute-done((bf16[64,320]{1,0:T(8,128)(2,1)S(1)}, bf16[64,320]{1,0:T(8,128)(2,1)S(1)}, u32[]{:S(2)}, u32[]{:S(2)}) %collective-permute-start.12) | collective-permute-done | bytes 40992 | tf_op jit(solution)/shard_map/ppermute | solution.py:21
  118.8 5.6 %collective-permute-done.13 = bf16[64,320]{1,0:T(8,128)(2,1)S(1)} collective-permute-done((bf16[64,320]{1,0:T(8,128)(2,1)S(1)}, bf16[64,320]{1,0:T(8,128)(2,1)S(1)}, u32[]{:S(2)}, u32[]{:S(2)}) %collective-permute-start.13) | collective-permute-done | bytes 40992 | tf_op jit(solution)/shard_map/ppermute | solution.py:21
  142.4 5.6 %copy.55 = bf16[5,8,16,8,512]{4,3,1,0,2:T(8,128)(2,1)} copy(bf16[5,8,16,8,512]{4,3,2,1,0:T(8,128)(2,1)} %bitcast.80) | data formatting | bytes 10485760 | tf_op jit(solution)/shard_map/reshape | solution.py:109
  148.0 5.6 %copy.56 = bf16[5,8,16,8,512]{4,3,1,0,2:T(8,128)(2,1)} copy(bf16[5,8,16,8,512]{4,3,2,1,0:T(8,128)(2,1)} %bitcast.81) | data formatting | bytes 10485760 | tf_op jit(solution)/shard_map/reshape | solution.py:108
  153.6 119.0 %while.18 = (s32[]{:T(128)}, f32[5,512]{1,0:T(8,128)S(1)}, f32[5,512]{1,0:T(8,128)S(1)}, f32[5,512,64]{1,2,0:T(8,128)S(1)}, s32[16]{0:T(128)S(1)}, /*index=5*/bf...) while((s32[]{:T(128)}, f32[5,512]{1,0:T(8,128)S(1)}, ...), condition=%wide.region_5.6_spmd.clone, body=%wide.region_2.5_spmd.clone.sunk | while | flops 384700416 | bytes 19313812 | solution.py:115
  158.5 2.5 fusion.83
  165.9 2.5 fusion.83
  173.3 2.5 fusion.83
  180.8 2.5 fusion.83
  188.2 2.5 fusion.83
  195.7 2.5 fusion.83
  203.1 2.5 fusion.83
  (230 shorter events, 118.6 us)
Async XLA Ops:
  6.5 1.0 copy-start
  6.5 135.9 %all-gather.5.cloned.1.call-start = ((), (), s32[]{:S(2)}) async-start(), calls=%async_computation.1 | async-start | bytes 5570560 | tf_op jit(solution)/shard_map/all_gather | solution.py:100
  9.6 138.4 %all-gather.3.cloned.1.call-start = ((), (), s32[]{:S(2)}) async-start(), calls=%async_computation | async-start | bytes 5570560 | tf_op jit(solution)/shard_map/all_gather | solution.py:99
  12.8 7.3 %collective-permute-start = (bf16[64,320]{1,0:T(8,128)(2,1)S(1)}, bf16[64,320]{1,0:T(8,128)(2,1)S(1)}, u32[]{:S(2)}, u32[]{:S(2)}) collective-permute-start(bf16[64,320]{1,0:T(8,128)(2,1)S(1)} %convolution_convert_fusion.5), channel_id=1, source_target_pairs={{0,1},{1,2},{2,3},{3,4},{4,5},{5,6},{6,7},{7,8},{8,9},{9,10},{10,1... | collective-permute-start | bytes 122888 | tf_op jit(solution)/shard_map/ppermute | solution.py:21
  20.1 6.8 %collective-permute-start.1 = (bf16[64,320]{1,0:T(8,128)(2,1)S(1)}, bf16[64,320]{1,0:T(8,128)(2,1)S(1)}, u32[]{:S(2)}, u32[]{:S(2)}) collective-permute-start(bf16[64,320]{1,0:T(8,128)(2,1)S(1)} %collective-permute-done), channel_id=1, source_target_pairs={{0,1},{1,2},{2,3},{3,4},{4,5},{5,6},{6,7},{7,8},{8,9},{9,10},{10,1... | collective-permute-start | bytes 122888 | tf_op jit(solution)/shard_map/ppermute | solution.py:21
  27.0 7.1 %collective-permute-start.2 = (bf16[64,320]{1,0:T(8,128)(2,1)S(1)}, bf16[64,320]{1,0:T(8,128)(2,1)S(1)}, u32[]{:S(2)}, u32[]{:S(2)}) collective-permute-start(bf16[64,320]{1,0:T(8,128)(2,1)S(1)} %collective-permute-done.1), channel_id=1, source_target_pairs={{0,1},{1,2},{2,3},{3,4},{4,5},{5,6},{6,7},{7,8},{8,9},{9,10},{10,1... | collective-permute-start | bytes 122888 | tf_op jit(solution)/shard_map/ppermute | solution.py:21
  34.0 6.2 %collective-permute-start.3 = (bf16[64,320]{1,0:T(8,128)(2,1)S(1)}, bf16[64,320]{1,0:T(8,128)(2,1)S(1)}, u32[]{:S(2)}, u32[]{:S(2)}) collective-permute-start(bf16[64,320]{1,0:T(8,128)(2,1)S(1)} %collective-permute-done.2), channel_id=1, source_target_pairs={{0,1},{1,2},{2,3},{3,4},{4,5},{5,6},{6,7},{7,8},{8,9},{9,10},{10,1... | collective-permute-start | bytes 122888 | tf_op jit(solution)/shard_map/ppermute | solution.py:21
  40.2 6.2 %collective-permute-start.4 = (bf16[64,320]{1,0:T(8,128)(2,1)S(1)}, bf16[64,320]{1,0:T(8,128)(2,1)S(1)}, u32[]{:S(2)}, u32[]{:S(2)}) collective-permute-start(bf16[64,320]{1,0:T(8,128)(2,1)S(1)} %collective-permute-done.3), channel_id=1, source_target_pairs={{0,1},{1,2},{2,3},{3,4},{4,5},{5,6},{6,7},{7,8},{8,9},{9,10},{10,1... | collective-permute-start | bytes 122888 | tf_op jit(solution)/shard_map/ppermute | solution.py:21
  46.4 7.4 %collective-permute-start.5 = (bf16[64,320]{1,0:T(8,128)(2,1)S(1)}, bf16[64,320]{1,0:T(8,128)(2,1)S(1)}, u32[]{:S(2)}, u32[]{:S(2)}) collective-permute-start(bf16[64,320]{1,0:T(8,128)(2,1)S(1)} %collective-permute-done.4), channel_id=1, source_target_pairs={{0,1},{1,2},{2,3},{3,4},{4,5},{5,6},{6,7},{7,8},{8,9},{9,10},{10,1... | collective-permute-start | bytes 122888 | tf_op jit(solution)/shard_map/ppermute | solution.py:21
  53.8 7.1 %collective-permute-start.6 = (bf16[64,320]{1,0:T(8,128)(2,1)S(1)}, bf16[64,320]{1,0:T(8,128)(2,1)S(1)}, u32[]{:S(2)}, u32[]{:S(2)}) collective-permute-start(bf16[64,320]{1,0:T(8,128)(2,1)S(1)} %collective-permute-done.5), channel_id=1, source_target_pairs={{0,1},{1,2},{2,3},{3,4},{4,5},{5,6},{6,7},{7,8},{8,9},{9,10},{10,1... | collective-permute-start | bytes 122888 | tf_op jit(solution)/shard_map/ppermute | solution.py:21
  60.9 7.2 %collective-permute-start.7 = (bf16[64,320]{1,0:T(8,128)(2,1)S(1)}, bf16[64,320]{1,0:T(8,128)(2,1)S(1)}, u32[]{:S(2)}, u32[]{:S(2)}) collective-permute-start(bf16[64,320]{1,0:T(8,128)(2,1)S(1)} %collective-permute-done.6), channel_id=1, source_target_pairs={{0,1},{1,2},{2,3},{3,4},{4,5},{5,6},{6,7},{7,8},{8,9},{9,10},{10,1... | collective-permute-start | bytes 122888 | tf_op jit(solution)/shard_map/ppermute | solution.py:21
  68.2 6.2 %collective-permute-start.8 = (bf16[64,320]{1,0:T(8,128)(2,1)S(1)}, bf16[64,320]{1,0:T(8,128)(2,1)S(1)}, u32[]{:S(2)}, u32[]{:S(2)}) collective-permute-start(bf16[64,320]{1,0:T(8,128)(2,1)S(1)} %collective-permute-done.7), channel_id=1, source_target_pairs={{0,1},{1,2},{2,3},{3,4},{4,5},{5,6},{6,7},{7,8},{8,9},{9,10},{10,1... | collective-permute-start | bytes 122888 | tf_op jit(solution)/shard_map/ppermute | solution.py:21
  74.4 6.2 %collective-permute-start.9 = (bf16[64,320]{1,0:T(8,128)(2,1)S(1)}, bf16[64,320]{1,0:T(8,128)(2,1)S(1)}, u32[]{:S(2)}, u32[]{:S(2)}) collective-permute-start(bf16[64,320]{1,0:T(8,128)(2,1)S(1)} %collective-permute-done.8), channel_id=1, source_target_pairs={{0,1},{1,2},{2,3},{3,4},{4,5},{5,6},{6,7},{7,8},{8,9},{9,10},{10,1... | collective-permute-start | bytes 122888 | tf_op jit(solution)/shard_map/ppermute | solution.py:21
  80.6 23.0 %collective-permute-start.10 = (bf16[64,320]{1,0:T(8,128)(2,1)S(1)}, bf16[64,320]{1,0:T(8,128)(2,1)S(1)}, u32[]{:S(2)}, u32[]{:S(2)}) collective-permute-start(bf16[64,320]{1,0:T(8,128)(2,1)S(1)} %collective-permute-done.9), channel_id=1, source_target_pairs={{0,1},{1,2},{2,3},{3,4},{4,5},{5,6},{6,7},{7,8},{8,9},{9,10},{10,1... | collective-permute-start | bytes 122888 | tf_op jit(solution)/shard_map/ppermute | solution.py:21
  103.6 6.2 %collective-permute-start.11 = (bf16[64,320]{1,0:T(8,128)(2,1)S(1)}, bf16[64,320]{1,0:T(8,128)(2,1)S(1)}, u32[]{:S(2)}, u32[]{:S(2)}) collective-permute-start(bf16[64,320]{1,0:T(8,128)(2,1)S(1)} %collective-permute-done.10), channel_id=1, source_target_pairs={{0,1},{1,2},{2,3},{3,4},{4,5},{5,6},{6,7},{7,8},{8,9},{9,10},{10,1... | collective-permute-start | bytes 122888 | tf_op jit(solution)/shard_map/ppermute | solution.py:21
  109.8 7.4 %collective-permute-start.12 = (bf16[64,320]{1,0:T(8,128)(2,1)S(1)}, bf16[64,320]{1,0:T(8,128)(2,1)S(1)}, u32[]{:S(2)}, u32[]{:S(2)}) collective-permute-start(bf16[64,320]{1,0:T(8,128)(2,1)S(1)} %collective-permute-done.11), channel_id=1, source_target_pairs={{0,1},{1,2},{2,3},{3,4},{4,5},{5,6},{6,7},{7,8},{8,9},{9,10},{10,1... | collective-permute-start | bytes 122888 | tf_op jit(solution)/shard_map/ppermute | solution.py:21
  117.2 7.2 %collective-permute-start.13 = (bf16[64,320]{1,0:T(8,128)(2,1)S(1)}, bf16[64,320]{1,0:T(8,128)(2,1)S(1)}, u32[]{:S(2)}, u32[]{:S(2)}) collective-permute-start(bf16[64,320]{1,0:T(8,128)(2,1)S(1)} %collective-permute-done.12), channel_id=1, source_target_pairs={{0,1},{1,2},{2,3},{3,4},{4,5},{5,6},{6,7},{7,8},{8,9},{9,10},{10,1... | collective-permute-start | bytes 122888 | tf_op jit(solution)/shard_map/ppermute | solution.py:21
  124.4 10.4 %collective-permute-start.14 = (bf16[64,320]{1,0:T(8,128)(2,1)S(1)}, bf16[64,320]{1,0:T(8,128)(2,1)S(1)}, u32[]{:S(2)}, u32[]{:S(2)}) collective-permute-start(bf16[64,320]{1,0:T(8,128)(2,1)S(1)} %collective-permute-done.13), channel_id=1, source_target_pairs={{0,1},{1,2},{2,3},{3,4},{4,5},{5,6},{6,7},{7,8},{8,9},{9,10},{10,1... | collective-permute-start | bytes 122888 | tf_op jit(solution)/shard_map/ppermute | solution.py:21
  153.6 119.0 %copy-start.1 = (bf16[320,320]{1,0:T(8,128)(2,1)S(1)}, bf16[320,320]{1,0:T(8,128)(2,1)}, u32[]{:S(2)}) copy-start(bf16[320,320]{1,0:T(8,128)(2,1)} %param.17) | copy-start | bytes 614404
Sparse Core Ops, SparseCore 0:
  9.7 64.7 all-gather.4
  76.6 61.9 all-gather.2
